TPU v7x, 32 devices: a whole 2x2x4 slice. The times are simulated.
32 devices in a mesh: shard: 2 (over x), ctx: 4 (over y, core), tp: 4 (over z).
Axes of the slice: x: 2, y: 2, z: 4, core: 2. Of those that a mesh axis runs over, the one named last changes fastest.
Arguments:
- hidden_in: bfloat16 [4, 1024, 1024], P('shard', 'ctx'), may hold values from -6 to 6
- lengths: int32 [4], P('shard'), may hold values from 1 to 1024, as said below
- cotangent: bfloat16 [4, 1024, 1024], P('shard', 'ctx'), may hold values from -6 to 6
- ln1_gain: bfloat16 [1024], P(('shard', 'ctx')), may hold values from 0.5 to 1.5
- ln1_bias: bfloat16 [1024], P(('shard', 'ctx')), may hold values from -3 to 3
- w_qkv: bfloat16 [3, 1024, 1024], P(None, ('shard', 'ctx'), 'tp'), may hold values from -0.1875 to 0.1875
- b_qv: bfloat16 [2, 1024], P(None, 'tp'), may hold values from -3 to 3
- w_out: bfloat16 [1024, 1024], P(('shard', 'ctx'), 'tp'), may hold values from -1.5 to 1.5
- b_out: bfloat16 [1024], P(('shard', 'ctx')), may hold values from -3 to 3
- ln2_gain: bfloat16 [1024], P(('shard', 'ctx')), may hold values from 0.5 to 1.5
- ln2_bias: bfloat16 [1024], P(('shard', 'ctx')), may hold values from -3 to 3
- w_up: bfloat16 [1024, 4096], P(('shard', 'ctx'), 'tp'), may hold values from -0.1875 to 0.1875
- b_up: bfloat16 [4096], P('tp'), may hold values from -3 to 3
- w_down: bfloat16 [1024, 4096], P(('shard', 'ctx'), 'tp'), may hold values from -0.375 to 0.375
- b_down: bfloat16 [1024], P(('shard', 'ctx')), may hold values from -3 to 3
Outputs:
- hidden_out: float32 [4, 1024, 1024], P('shard', 'ctx')
- grad_in: float32 [4, 1024, 1024], P('shard', 'ctx')
- grad_ln1_gain: float32 [1024], P(('shard', 'ctx'))
- grad_ln1_bias: float32 [1024], P(('shard', 'ctx'))
- grad_w_qkv: float32 [3, 1024, 1024], P(None, ('shard', 'ctx'), 'tp')
- grad_b_qv: float32 [2, 1024], P(None, 'tp')
- grad_w_out: float32 [1024, 1024], P(('shard', 'ctx'), 'tp')
- grad_b_out: float32 [1024], P(('shard', 'ctx'))
- grad_ln2_gain: float32 [1024], P(('shard', 'ctx'))
- grad_ln2_bias: float32 [1024], P(('shard', 'ctx'))
- grad_w_up: float32 [1024, 4096], P(('shard', 'ctx'), 'tp')
- grad_b_up: float32 [4096], P('tp')
- grad_w_down: float32 [1024, 4096], P(('shard', 'ctx'), 'tp')
- grad_b_down: float32 [1024], P(('shard', 'ctx'))
Inputs may be any that keep to these rules, and one draw needn't show every extreme that they name: Sequence i belongs to shard group i // 2; its positions from lengths[i] on are padding. Some sequence has all 1024 positions live.
All inputs are finite; a program needn't handle non-finite values.
Results may differ from a plain program's by a relative error of at most 0.012.
The roundings to bfloat16 on the way count: a program that leaves them out, or rounds other values in their place, can miss the bound.
Values may be sent and summed in bfloat16 or wider, within the bound.
A program may use at most 128 MiB of HBM per device.

v0:
```python
import math
import jax
import jax.numpy as jnp
from jax import lax
from jax.sharding import PartitionSpec as P

HD = 64
EPS = 1e-05
KAPPA = math.sqrt(2.0 / math.pi)


def normalize(row, gain, shift):
    center = jnp.mean(row, axis=-1, keepdims=True)
    centred = row - center
    inv_std = lax.rsqrt(jnp.mean(centred * centred, axis=-1, keepdims=True) + EPS)
    unit_rows = centred * inv_std
    return (unit_rows * gain + shift, unit_rows, inv_std)


def normalize_back(grad_out, unit_rows, inv_std, gain):
    scaled = grad_out * gain
    return inv_std * (
        scaled
        - jnp.mean(scaled, axis=-1, keepdims=True)
        - unit_rows * jnp.mean(scaled * unit_rows, axis=-1, keepdims=True)
    )


def gelu_pair(pre_act):
    inner = KAPPA * (pre_act + 0.044715 * pre_act * pre_act * pre_act)
    tanh_val = jnp.tanh(inner)
    value_out = 0.5 * pre_act * (1.0 + tanh_val)
    slope = 0.5 * (1.0 + tanh_val) + 0.5 * pre_act * (1.0 - tanh_val * tanh_val) * KAPPA * (
        1.0 + 3.0 * 0.044715 * pre_act * pre_act
    )
    return (value_out, slope)


def contract_last(left, right):
    return lax.dot_general(
        left, right, (((1,), (1,)), ((), ())), preferred_element_type=jnp.float32
    )


def contract_first(left, right):
    return lax.dot_general(
        left, right, (((0,), (0,)), ((), ())), preferred_element_type=jnp.float32
    )


def on_device(
    hidden_in,
    lengths,
    cotangent,
    ln1_gain,
    ln1_bias,
    w_qkv,
    b_qv,
    w_out,
    b_out,
    ln2_gain,
    ln2_bias,
    w_up,
    b_up,
    w_down,
    b_down,
):
    groups, block_len, width = hidden_in.shape
    head_width = w_qkv.shape[2]
    heads_here = head_width // HD
    row_count = groups * block_len
    scale = 1.0 / math.sqrt(HD)
    vectors = jnp.stack([ln1_gain, ln1_bias, b_out, ln2_gain, ln2_bias, b_down], 0)
    fetched = (
        lax.all_gather(w_qkv, ("shard", "ctx"), axis=1, tiled=True),
        lax.all_gather(w_out, ("shard", "ctx"), axis=0, tiled=True),
        lax.all_gather(w_up, ("shard", "ctx"), axis=0, tiled=True),
        lax.all_gather(w_down, ("shard", "ctx"), axis=0, tiled=True),
        lax.all_gather(vectors, ("shard", "ctx"), axis=1, tiled=True),
    )
    qkv_full, out_full, up_full, down_full, vec_full = fetched
    vec_wide = vec_full.astype(jnp.float32)
    gain_one = vec_wide[0]
    shift_one = vec_wide[1]
    bias_out = vec_wide[2]
    gain_two = vec_wide[3]
    shift_two = vec_wide[4]
    bias_down = vec_wide[5]
    ctx_index = lax.axis_index("ctx")
    positions = jnp.arange(block_len, dtype=jnp.int32) + ctx_index * block_len
    live_rows = (positions[None, :] < lengths[:, None]).reshape(row_count, 1)

    def allowed_mask(start, count):
        key_pos = start + jnp.arange(count, dtype=jnp.int32)
        causal = key_pos[None, None, None, :] <= positions[None, None, :, None]
        inside = key_pos[None, None, None, :] < lengths[:, None, None, None]
        return causal & inside

    inputs = hidden_in.reshape(row_count, width).astype(jnp.float32)
    normed_one, unit_one, inv_one = normalize(inputs, gain_one, shift_one)
    normed_bf = normed_one.astype(jnp.bfloat16)
    projected = jnp.einsum("rd,jde->jre", normed_bf, qkv_full, preferred_element_type=jnp.float32)
    query = (projected[0] + b_qv[0].astype(jnp.float32)).astype(jnp.bfloat16)
    keys_here = projected[1].astype(jnp.bfloat16).reshape(groups, block_len, head_width)
    values_here = (
        (projected[2] + b_qv[1].astype(jnp.float32))
        .astype(jnp.bfloat16)
        .reshape(groups, block_len, head_width)
    )
    query_heads = query.reshape(groups, block_len, heads_here, HD)

    def fold_keys(step_fn, init):
        return step_fn(
            init,
            (
                lax.all_gather(keys_here, "ctx", axis=1, tiled=True),
                lax.all_gather(values_here, "ctx", axis=1, tiled=True),
            ),
            jnp.int32(0),
        )

    def piece_scores(piece, start):
        key_piece, value_piece = piece
        count = key_piece.shape[1]
        key_heads = key_piece.reshape(groups, count, heads_here, HD)
        value_heads = value_piece.reshape(groups, count, heads_here, HD)
        scores = (
            jnp.einsum(
                "sqhd,skhd->shqk", query_heads, key_heads, preferred_element_type=jnp.float32
            )
            * scale
        )
        allowed = allowed_mask(start, count)
        return (jnp.where(allowed, scores, -1e30), allowed, value_heads)

    def totals_step(carry, piece, start):
        top, total = carry
        scores, allowed, unused = piece_scores(piece, start)
        new_top = jnp.maximum(top, jnp.max(scores, axis=-1))
        weights = jnp.where(allowed, jnp.exp(scores - new_top[..., None]), 0.0)
        total = jnp.sum(weights, axis=-1)
        return (new_top, total)

    start_totals = (
        jnp.full((groups, heads_here, block_len), -1e30, jnp.float32),
        jnp.zeros((groups, heads_here, block_len), jnp.float32),
    )
    top, total = fold_keys(totals_step, start_totals)
    log_total = top + jnp.log(total)

    def values_step(accum, piece, start):
        scores, allowed, value_heads = piece_scores(piece, start)
        probs_piece = jnp.where(allowed, jnp.exp(scores - log_total[..., None]), 0.0).astype(
            jnp.bfloat16
        )
        return jnp.einsum(
            "shqk,skhd->sqhd", probs_piece, value_heads, preferred_element_type=jnp.float32
        )

    accum = fold_keys(values_step, jnp.zeros((groups, block_len, heads_here, HD), jnp.float32))
    attended_heads = accum.astype(jnp.bfloat16)
    attended = attended_heads.reshape(row_count, head_width)
    proj_sum = lax.psum(contract_last(attended, out_full), "tp")
    resid = inputs + proj_sum + bias_out
    normed_two, unit_two, inv_two = normalize(resid, gain_two, shift_two)
    second_bf = normed_two.astype(jnp.bfloat16)
    pre_act = jnp.dot(second_bf, up_full, preferred_element_type=jnp.float32) + b_up.astype(
        jnp.float32
    )
    activ, slope = gelu_pair(pre_act)
    hidden = activ.astype(jnp.bfloat16)
    mlp_sum = lax.psum(contract_last(hidden, down_full), "tp")
    result = jnp.where(live_rows, resid + mlp_sum + bias_down, 0.0)
    again = (
        lax.all_gather(w_qkv, ("shard", "ctx"), axis=1, tiled=True),
        lax.all_gather(w_out, ("shard", "ctx"), axis=0, tiled=True),
        lax.all_gather(w_up, ("shard", "ctx"), axis=0, tiled=True),
        lax.all_gather(w_down, ("shard", "ctx"), axis=0, tiled=True),
    )
    qkv_back, out_back, up_back, down_back = again
    grad_rows = jnp.where(live_rows, cotangent.reshape(row_count, width).astype(jnp.float32), 0.0)
    grad_bf = grad_rows.astype(jnp.bfloat16)
    grad_bias_down = jnp.sum(grad_rows, axis=0)
    grad_down = contract_first(grad_bf, hidden)
    d_pre = jnp.dot(grad_bf, down_back, preferred_element_type=jnp.float32) * slope
    d_pre_bf = d_pre.astype(jnp.bfloat16)
    grad_bias_up = jnp.sum(d_pre, axis=0)
    grad_up = contract_first(second_bf, d_pre_bf)
    back_two = lax.psum(contract_last(d_pre_bf, up_back), "tp")
    grad_gain_two = jnp.sum(back_two * unit_two, axis=0)
    grad_shift_two = jnp.sum(back_two, axis=0)
    d_resid = grad_rows + normalize_back(back_two, unit_two, inv_two, gain_two)
    d_resid_bf = d_resid.astype(jnp.bfloat16)
    grad_bias_out = jnp.sum(d_resid, axis=0)
    grad_out = contract_first(d_resid_bf, attended)
    d_attended = jnp.dot(d_resid_bf, out_back, preferred_element_type=jnp.float32).astype(
        jnp.bfloat16
    )
    keys_whole, values_whole = (
        lax.all_gather(keys_here, "ctx", axis=1, tiled=True),
        lax.all_gather(values_here, "ctx", axis=1, tiled=True),
    )
    seq_len = keys_whole.shape[1]
    key_heads = keys_whole.reshape(groups, seq_len, heads_here, HD)
    value_heads = values_whole.reshape(groups, seq_len, heads_here, HD)
    scores = (
        jnp.einsum("sqhd,skhd->shqk", query_heads, key_heads, preferred_element_type=jnp.float32)
        * scale
    )
    allowed = allowed_mask(0, seq_len)
    exact_probs = jnp.where(allowed, jnp.exp(scores - log_total[..., None]), 0.0)
    d_att_heads = d_attended.reshape(groups, block_len, heads_here, HD)
    delta = jnp.transpose(
        jnp.sum(d_att_heads.astype(jnp.float32) * attended_heads.astype(jnp.float32), axis=-1),
        (0, 2, 1),
    )
    d_probs = jnp.einsum(
        "sqhd,skhd->shqk", d_att_heads, value_heads, preferred_element_type=jnp.float32
    )
    d_scores = (exact_probs * (d_probs - delta[..., None])).astype(jnp.bfloat16)
    d_query = (
        jnp.einsum("shqk,skhd->sqhd", d_scores, key_heads, preferred_element_type=jnp.float32)
        * scale
    )
    probs_bf = exact_probs.astype(jnp.bfloat16)
    key_terms = (
        jnp.einsum("shqk,sqhd->skhd", d_scores, query_heads, preferred_element_type=jnp.float32)
        * scale
    )
    value_terms = jnp.einsum(
        "shqk,sqhd->skhd", probs_bf, d_att_heads, preferred_element_type=jnp.float32
    )
    d_keys, d_values = (
        lax.psum_scatter(
            key_terms.reshape(groups, seq_len, head_width), "ctx", scatter_dimension=1, tiled=True
        ),
        lax.psum_scatter(
            value_terms.reshape(groups, seq_len, head_width), "ctx", scatter_dimension=1, tiled=True
        ),
    )
    d_query_rows = d_query.reshape(row_count, head_width)
    d_value_rows = d_values.reshape(row_count, head_width)
    grad_bias_qv = jnp.stack([jnp.sum(d_query_rows, axis=0), jnp.sum(d_value_rows, axis=0)], 0)
    stacked = jnp.stack(
        [d_query_rows, d_keys.reshape(row_count, head_width), d_value_rows], 0
    ).astype(jnp.bfloat16)
    grad_qkv = jnp.einsum("rd,jre->jde", normed_bf, stacked, preferred_element_type=jnp.float32)
    back_one = lax.psum(
        jnp.einsum("jre,jde->rd", stacked, qkv_back, preferred_element_type=jnp.float32), "tp"
    )
    grad_gain_one = jnp.sum(back_one * unit_one, axis=0)
    grad_shift_one = jnp.sum(back_one, axis=0)
    d_inputs = d_resid + normalize_back(back_one, unit_one, inv_one, gain_one)
    vec_grads = jnp.stack(
        [
            grad_gain_one,
            grad_shift_one,
            grad_bias_out,
            grad_gain_two,
            grad_shift_two,
            grad_bias_down,
        ],
        0,
    )
    summed = (
        lax.psum_scatter(grad_qkv, ("shard", "ctx"), scatter_dimension=1, tiled=True),
        lax.psum_scatter(grad_out, ("shard", "ctx"), scatter_dimension=0, tiled=True),
        lax.psum_scatter(grad_up, ("shard", "ctx"), scatter_dimension=0, tiled=True),
        lax.psum_scatter(grad_down, ("shard", "ctx"), scatter_dimension=0, tiled=True),
        lax.psum_scatter(vec_grads, ("shard", "ctx"), scatter_dimension=1, tiled=True),
    )
    sum_qkv, sum_out, sum_up, sum_down, sum_vec = summed
    bias_qv_sum, bias_up_sum = lax.psum((grad_bias_qv, grad_bias_up), ("shard", "ctx"))
    return (
        result.reshape(groups, block_len, width),
        d_inputs.reshape(groups, block_len, width),
        sum_vec[0],
        sum_vec[1],
        sum_qkv,
        bias_qv_sum,
        sum_out,
        sum_vec[2],
        sum_vec[3],
        sum_vec[4],
        sum_up,
        bias_up_sum,
        sum_down,
        sum_vec[5],
    )


def solution(mesh):
    return jax.shard_map(
        on_device,
        mesh=mesh,
        in_specs=(
            P("shard", "ctx", None),
            P("shard"),
            P("shard", "ctx", None),
            P(("shard", "ctx")),
            P(("shard", "ctx")),
            P(None, ("shard", "ctx"), "tp"),
            P(None, "tp"),
            P(("shard", "ctx"), "tp"),
            P(("shard", "ctx")),
            P(("shard", "ctx")),
            P(("shard", "ctx")),
            P(("shard", "ctx"), "tp"),
            P("tp"),
            P(("shard", "ctx"), "tp"),
            P(("shard", "ctx")),
        ),
        out_specs=(
            P("shard", "ctx", None),
            P("shard", "ctx", None),
            P(("shard", "ctx")),
            P(("shard", "ctx")),
            P(None, ("shard", "ctx"), "tp"),
            P(None, "tp"),
            P(("shard", "ctx"), "tp"),
            P(("shard", "ctx")),
            P(("shard", "ctx")),
            P(("shard", "ctx")),
            P(("shard", "ctx"), "tp"),
            P("tp"),
            P(("shard", "ctx"), "tp"),
            P(("shard", "ctx")),
        ),
        check_vma=False,
    )
```

profile of v0, /device:TPU:0, one launch (start us, length us, event | category | flops | bytes accessed | tf_op | source)
XLA Modules:
  0.0 817.6 jit_solution(358480449158023805)
XLA Ops:
  11.3 10.3 %all_gather.28 = bf16[6,1024]{1,0:T(8,128)(2,1)S(1)} all-gather(bf16[6,128]{1,0:T(8,128)(2,1)S(1)} %stack.61), channel_id=1, replica_groups=mesh['shard'=2,'ctx'=4,'tp'=4] {'shard','ctx'}, dimensions={1}, use_global_device_ids=true | all-gather | bytes 13824 | tf_op jit(solution)/shard_map/all_gather | solution.py:79
  23.1 15.3 %all-gather.6.cloned.1.call-done = bf16[3,1024,256]{2,1,0:T(8,128)(2,1)} async-done(((bf16[3,128,256]{2,1,0:T(8,128)(2,1)}), bf16[3,1024,256]{2,1,0:T(8,128)(2,1)}) %all-gather.6.cloned.1.call-update) | async-done | bytes 1572880 | tf_op jit(solution)/shard_map/all_gather | solution.py:75
  38.4 2.7 convolution_bitcast_fusion.2
  42.1 10.8 %all_gather.32 = bf16[1024,256]{1,0:T(8,128)(2,1)} all-gather(bf16[128,256]{1,0:T(8,128)(2,1)S(1)} %copy-done.20), channel_id=1, replica_groups=mesh['shard'=2,'ctx'=4,'tp'=4] {'shard','ctx'}, dimensions={0}, use_global_device_ids=true | all-gather | bytes 589824 | tf_op jit(solution)/shard_map/all_gather | solution.py:76
  53.5 2.3 fusion.56
  56.5 2.0 add_convert_fusion.2
  60.3 1.8 fusion
  62.2 3.0 select_reduce_fusion
  65.4 12.3 %all-gather.8.cloned.1.call-done = bf16[2,1024,256]{2,1,0:T(8,128)(2,1)} async-done(((bf16[2,256,256]{2,1,0:T(8,128)(2,1)}), bf16[2,1024,256]{2,1,0:T(8,128)(2,1)}) %all-gather.8.cloned.1.call-update) | async-done | bytes 1048592 | tf_op jit(solution)/shard_map/all_gather | solution.py:117
  79.3 6.0 fusion.31
  86.0 1.8 fusion.61
  90.5 83.9 %all-reduce.6.cloned.1.call-done = f32[512,1024]{1,0:T(8,128)} async-done(((f32[512,1024]{1,0:T(8,128)}), f32[512,1024]{1,0:T(8,128)}) %all-reduce.6.cloned.1.call-update) | async-done | bytes 2097168 | tf_op jit(solution)/shard_map/psum | solution.py:163
  174.5 1.9 fusion.54
  176.8 26.5 %all-gather.12.cloned.1.call-done = bf16[1024,1024]{1,0:T(8,128)(2,1)} async-done(((bf16[128,1024]{1,0:T(8,128)(2,1)}), bf16[1024,1024]{1,0:T(8,128)(2,1)}) %all-gather.12.cloned.1.call-update) | async-done | bytes 2097168 | tf_op jit(solution)/shard_map/all_gather | solution.py:77
  203.3 4.2 fusion.52
  207.5 25.6 %all-gather.14.cloned.1.call-done = bf16[1024,1024]{1,0:T(8,128)(2,1)} async-done(((bf16[128,1024]{1,0:T(8,128)(2,1)}), bf16[1024,1024]{1,0:T(8,128)(2,1)}) %all-gather.14.cloned.1.call-update) | async-done | bytes 2097168 | tf_op jit(solution)/shard_map/all_gather | solution.py:78
  233.1 5.0 fusion.60
  239.2 2.6 fusion.39
  241.9 86.6 %all-reduce.8.cloned.1.call-done = f32[512,1024]{1,0:T(8,128)} async-done(((f32[512,1024]{1,0:T(8,128)}), f32[512,1024]{1,0:T(8,128)}) %all-reduce.8.cloned.1.call-update) | async-done | bytes 2097168 | tf_op jit(solution)/shard_map/psum | solution.py:189
  328.5 2.6 multiply_reduce_fusion
  334.7 2.0 reshape.250
  336.8 2.0 copy.58
  339.8 6.1 multiply_convert_fusion
  346.0 2.6 convolution_multiply_fusion
  348.7 6.8 fusion.2
  355.8 5.3 fusion.51
  361.1 2.1 fusion.57
  363.2 2.0 copy.70
  365.2 2.2 reshape.249
  367.3 11.8 %reduce-scatter.8.cloned.1.call-done = f32[2,256,256]{1,2,0:T(8,128)} async-done(((f32[2,1024,256]{1,2,0:T(8,128)}), f32[2,256,256]{1,2,0:T(8,128)}) %reduce-scatter.8.cloned.1.call-update) | async-done | bytes 524304 | tf_op jit(solution)/shard_map/reduce_scatter | solution.py:234
  380.9 1.8 copy.61
  382.7 30.6 %reduce-scatter.10.cloned.1.call-done = f32[2,256,256]{1,2,0:T(8,128)} async-done(((f32[2,1024,256]{1,2,0:T(8,128)}), f32[2,256,256]{1,2,0:T(8,128)}) %reduce-scatter.10.cloned.1.call-update) | async-done | bytes 524304 | tf_op jit(solution)/shard_map/reduce_scatter | solution.py:237
  413.4 2.0 fusion.58
  417.1 4.0 convolution_bitcast_fusion.1
  422.7 153.9 %all-reduce.10.cloned.1.call-done = (f32[512,1024]{1,0:T(8,128)}, f32[512,1024]{1,0:T(8,128)}) async-done(((f32[512,1024]{1,0:T(8,128)}, f32[512,1024]{1,0:T(8,128)}), (f32[512,1024]{1,0:T(8,128)}, f32[512,1024]{1,0:T(8,128)})) %all-reduce.10.cloned.1.call-update) | async-done | bytes 4194320 | tf_op jit(solution)/shard_map/psum | solution.py:172
  576.7 2.5 fusion.26
  579.9 4.3 convolution_bitcast_fusion
  584.2 3.1 fusion.34
  587.4 5.3 fusion.50
  592.7 4.6 fusion.37
  597.5 14.4 %all-reduce = (f32[2,256]{1,0:T(2,128)}, f32[1024]{0:T(1024)}) all-reduce(f32[2,256]{1,0:T(2,128)S(1)} %pad_maximum_fusion.3, f32[1024]{0:T(1024)S(1)} %get-tuple-element.95), channel_id=1, replica_groups=mesh['shard'=2,'ctx'=4,'tp'=4] {'shard','ctx'}, use_global_device_ids=true, to_apply=%region_27.28 | all-reduce | flops 1536 | bytes 12288 | tf_op jit(solution)/shard_map/psum | solution.py:273
  611.9 3.3 add_select_fusion
  615.3 2.0 fusion.25
  618.7 41.6 %reduce-scatter.14.cloned.1.call-done = f32[3,128,256]{1,2,0:T(8,128)} async-done(((f32[3,1024,256]{1,2,0:T(8,128)}), f32[3,128,256]{1,2,0:T(8,128)}) %reduce-scatter.14.cloned.1.call-update) | async-done | bytes 393232 | tf_op jit(solution)/shard_map/reduce_scatter | solution.py:266
  660.3 1.9 copy.66
  662.2 38.2 %reduce-scatter.16.cloned.1.call-done = f32[128,256]{1,0:T(8,128)} async-done(((f32[1024,256]{1,0:T(8,128)}), f32[128,256]{1,0:T(8,128)}) %reduce-scatter.16.cloned.1.call-update) | async-done | bytes 131088 | tf_op jit(solution)/shard_map/reduce_scatter | solution.py:267
  700.4 55.5 %reduce-scatter.20.cloned.1.call-done = f32[128,1024]{1,0:T(8,128)} async-done(((f32[1024,1024]{1,0:T(8,128)}), f32[128,1024]{1,0:T(8,128)}) %reduce-scatter.20.cloned.1.call-update) | async-done | bytes 524304 | tf_op jit(solution)/shard_map/reduce_scatter | solution.py:269
  755.9 55.1 %reduce-scatter.18.cloned.1.call-done = f32[128,1024]{1,0:T(8,128)} async-done(((f32[1024,1024]{1,0:T(8,128)}), f32[128,1024]{1,0:T(8,128)}) %reduce-scatter.18.cloned.1.call-update) | async-done | bytes 524304 | tf_op jit(solution)/shard_map/reduce_scatter | solution.py:268
  (141 shorter events, 28.7 us)
Async XLA Ops:
  7.2 14.5 %copy-start = (bf16[2,256,1024]{2,1,0:T(8,128)(2,1)S(1)}, bf16[2,256,1024]{2,1,0:T(8,128)(2,1)}, u32[]{:S(2)}) copy-start(bf16[2,256,1024]{2,1,0:T(8,128)(2,1)} %param.15) | copy-start | bytes 3145732
  7.2 4.0 copy-start.29
  7.2 4.0 copy-start.28
  7.2 4.0 copy-start.27
  7.2 4.0 copy-start.26
  7.2 4.0 copy-start.25
  7.2 4.0 copy-start.24
  7.3 14.4 %copy-start.21 = (bf16[2,256]{1,0:T(2,128)(2,1)S(1)}, bf16[2,256]{1,0:T(2,128)(2,1)}, u32[]{:S(2)}) copy-start(bf16[2,256]{1,0:T(2,128)(2,1)} %param.21) | copy-start | bytes 3076
  7.3 31.2 %all-gather.6.cloned.1.call-start = ((), (), s32[]{:S(2)}) async-start(), calls=%async_computation.7 | async-start | bytes 1769472 | tf_op jit(solution)/shard_map/all_gather | solution.py:75
  8.0 50.8 %all-gather.10.cloned.1.call-start = ((), (), s32[]{:S(2)}) async-start(), calls=%async_computation.9 | async-start | bytes 1310720 | tf_op jit(solution)/shard_map/all_gather | solution.py:116
  23.1 19.0 %copy-start.20 = (bf16[128,256]{1,0:T(8,128)(2,1)S(1)}, bf16[128,256]{1,0:T(8,128)(2,1)}, u32[]{:S(2)}) copy-start(bf16[128,256]{1,0:T(8,128)(2,1)} %param.22) | copy-start | bytes 196612
  23.1 29.8 %copy-start.23 = (s32[2]{0:T(128)S(1)}, s32[2]{0:T(128)}, u32[]{:S(2)}) copy-start(s32[2]{0:T(128)} %param.16) | copy-start | bytes 28
  41.1 12.0 %copy-start.17 = (f32[3,512,256]{2,1,0:T(8,128)}, f32[3,512,256]{2,1,0:T(8,128)S(1)}, u32[]{:S(2)}) copy-start(f32[3,512,256]{2,1,0:T(8,128)S(1)} %convolution_bitcast_fusion.2) | copy-start | bytes 4718596
  42.0 35.8 %all-gather.8.cloned.1.call-start = ((), (), s32[]{:S(2)}) async-start(), calls=%async_computation.8 | async-start | bytes 1310720 | tf_op jit(solution)/shard_map/all_gather | solution.py:117
  53.4 25.8 %copy-start.14 = (pred[2,256,1024]{2,1,0:T(8,128)(4,1)}, pred[2,256,1024]{2,1,0:T(8,128)(4,1)S(1)}, u32[]{:S(2)}) copy-start(pred[2,256,1024]{2,1,0:T(8,128)(4,1)S(1)} %broadcast_and_fusion) | copy-start | bytes 1572868
  56.5 5.7 copy-start.12
  58.5 116.0 %all-reduce.6.cloned.1.call-start = ((), (), s32[]{:S(2)}) async-start(), calls=%async_computation.10 | async-start | bytes 4194304 | tf_op jit(solution)/shard_map/psum | solution.py:163
  60.3 1.9 copy-start.8
  62.2 3.2 copy-start.1
  79.2 6.0 copy-start.18
  79.3 6.7 copy-start.15
  85.3 0.7 copy-start.19
  86.0 3.3 copy-start.22
  86.0 3.3 copy-start.6
  87.8 115.4 %all-gather.12.cloned.1.call-start = ((), (), s32[]{:S(2)}) async-start(), calls=%async_computation.11 | async-start | bytes 2359296 | tf_op jit(solution)/shard_map/all_gather | solution.py:77
  88.4 144.7 %all-gather.14.cloned.1.call-start = ((), (), s32[]{:S(2)}) async-start(), calls=%async_computation.12 | async-start | bytes 2359296 | tf_op jit(solution)/shard_map/all_gather | solution.py:78
  89.0 239.5 %all-reduce.8.cloned.1.call-start = ((), (), s32[]{:S(2)}) async-start(), calls=%async_computation.13 | async-start | bytes 4194304 | tf_op jit(solution)/shard_map/psum | solution.py:189
  233.1 6.1 copy-start.30
  238.1 1.1 copy-start.31
  241.8 137.4 %reduce-scatter.8.cloned.1.call-start = ((), (), s32[]{:S(2)}) async-start(), calls=%async_computation.14 | async-start | bytes 2621440 | tf_op jit(solution)/shard_map/reduce_scatter | solution.py:234
  328.5 2.6 copy-start.7
  328.5 2.6 copy-start.10
  331.1 2.5 copy-start.16
  332.2 1.4 copy-start.2
  339.8 6.1 copy-start.13
  346.0 2.7 copy-start.4
  348.6 64.7 %reduce-scatter.10.cloned.1.call-start = ((), (), s32[]{:S(2)}) async-start(), calls=%async_computation.15 | async-start | bytes 2621440 | tf_op jit(solution)/shard_map/reduce_scatter | solution.py:237
  355.5 221.2 %all-reduce.10.cloned.1.call-start = ((), (), s32[]{:S(2)}) async-start(), calls=%async_computation.21 | async-start | bytes 8388608 | tf_op jit(solution)/shard_map/psum | solution.py:172
  355.7 5.4 copy-start.5
  355.7 5.3 copy-start.9
  421.2 196.1 %reduce-scatter.12.cloned.1.call-start = ((), (), s32[]{:S(2)}) async-start(), calls=%async_computation.16 | async-start | bytes 36864 | tf_op jit(solution)/shard_map/reduce_scatter | solution.py:270
  579.9 80.5 %reduce-scatter.14.cloned.1.call-start = ((), (), s32[]{:S(2)}) async-start(), calls=%async_computation.17 | async-start | bytes 3538944 | tf_op jit(solution)/shard_map/reduce_scatter | solution.py:266
  584.2 116.3 %reduce-scatter.16.cloned.1.call-start = ((), (), s32[]{:S(2)}) async-start(), calls=%async_computation.18 | async-start | bytes 1179648 | tf_op jit(solution)/shard_map/reduce_scatter | solution.py:267
  587.3 168.6 %reduce-scatter.20.cloned.1.call-start = ((), (), s32[]{:S(2)}) async-start(), calls=%async_computation.20 | async-start | bytes 4718592 | tf_op jit(solution)/shard_map/reduce_scatter | solution.py:269
  592.7 218.4 %reduce-scatter.18.cloned.1.call-start = ((), (), s32[]{:S(2)}) async-start(), calls=%async_computation.19 | async-start | bytes 4718592 | tf_op jit(solution)/shard_map/reduce_scatter | solution.py:268
  611.9 3.3 copy-start.3
  611.9 3.3 copy-start.11
Sparse Core Ops, SparseCore 0:
  10.0 28.3 all-gather.5
  42.1 16.7 all-gather.9
  61.0 16.7 all-gather.7
  87.9 86.4 all-reduce.5
  176.4 26.8 all-gather.11
  205.2 27.8 all-gather.13
  241.9 86.5 all-reduce.7
  348.8 30.3 reduce-scatter.7
  381.9 31.4 reduce-scatter.9
  421.3 155.3 all-reduce.9
  580.5 30.2 reduce-scatter.11
  614.0 46.2 reduce-scatter.13
  664.4 36.0 reduce-scatter.15
  704.6 51.2 reduce-scatter.19
  759.7 51.3 reduce-scatter.17
where the time goes:
time: 819 us; the launch traced here: 818 us
  waiting for transfers between devices  639 us (78%)
  matrix products  69.5 us (8%)
  blocking collectives  35.5 us (4%)
  other arithmetic  31.6 us (4%)
  local copies, waits for them, and re-layouts  26.2 us (3%)
  between operations  14.5 us (2%)
    psum x1, waiting for transfers between devices, on_device(): mlp_sum = lax.psum(contract_last(hidden, down_full), 'tp')  154 us
    psum x1, waiting for transfers between devices, on_device(): back_two = lax.psum(contract_last(d_pre_bf, up_back), 'tp')  86.6 us
    psum x1, waiting for transfers between devices, on_device(): proj_sum = lax.psum(contract_last(attended, out_full), 'tp')  83.9 us
    reduce_scatter x1, waiting for transfers between devices, on_device(): lax.psum_scatter(grad_down, ('shard', 'ctx'), scatter_dimension=0, tiled=...  55.5 us
    reduce_scatter x1, waiting for transfers between devices, on_device(): lax.psum_scatter(grad_up, ('shard', 'ctx'), scatter_dimension=0, tiled=True)  55.1 us
    reduce_scatter x1, waiting for transfers between devices, on_device(): lax.psum_scatter(grad_qkv, ('shard', 'ctx'), scatter_dimension=1, tiled=T...  41.6 us
    reduce_scatter x1, waiting for transfers between devices, on_device(): lax.psum_scatter(grad_out, ('shard', 'ctx'), scatter_dimension=0, tiled=T...  38.2 us
    reduce_scatter x1, waiting for transfers between devices, on_device(): lax.psum_scatter(value_terms.reshape(groups, seq_len, head_width), 'ctx',...  30.6 us
  transfers between devices with their start and end apart: 15, of which 14 were waited for; matrix products, arithmetic and copies ran while one was open for 9% of the time, Pallas kernels for 0%

commit v1 on v0

--- a/solution.py
+++ b/solution.py
@@ -7,6 +7,22 @@
 HD = 64
 EPS = 1e-05
 KAPPA = math.sqrt(2.0 / math.pi)
+
+
+def collect(x, axis, dim):
+    ways, here, step = (lax.axis_size(axis), lax.axis_index(axis), x.shape[dim])
+    shape = [n * ways if d == dim else n for d, n in enumerate(x.shape)]
+    full = lax.dynamic_update_slice_in_dim(jnp.zeros(shape, x.dtype), x, here * step, axis=dim)
+    going_up = going_down = x
+    for far in range(1, ways // 2 + 1):
+        going_up = lax.ppermute(going_up, axis, [(d, (d + 1) % ways) for d in range(ways)])
+        full = lax.dynamic_update_slice_in_dim(full, going_up, (here - far) % ways * step, axis=dim)
+        if 2 * far < ways:
+            going_down = lax.ppermute(going_down, axis, [(d, (d - 1) % ways) for d in range(ways)])
+            full = lax.dynamic_update_slice_in_dim(
+                full, going_down, (here + far) % ways * step, axis=dim
+            )
+    return full
 
 
 def normalize(row, gain, shift):
@@ -74,7 +90,7 @@
     fetched = (
         lax.all_gather(w_qkv, ("shard", "ctx"), axis=1, tiled=True),
         lax.all_gather(w_out, ("shard", "ctx"), axis=0, tiled=True),
-        lax.all_gather(w_up, ("shard", "ctx"), axis=0, tiled=True),
+        collect(w_up, ("shard", "ctx"), 0),
         lax.all_gather(w_down, ("shard", "ctx"), axis=0, tiled=True),
         lax.all_gather(vectors, ("shard", "ctx"), axis=1, tiled=True),
     )

time: 819 us -> 815 us (level)
  waiting for transfers between devices: 639 us -> 622 us
    psum x1, waiting for transfers between devices: 83.9 us -> 57.6 us  [on_device(): proj_sum = lax.psum(contract_last(attended, out_full), 'tp')]
    ppermute x0 -> x7, waiting for transfers between devices: none -> 13 us  [the longest x4 12.1 us: collect(): lax.ppermute(going_up, axis, [(d, (d + 1) % ways) for d in range(ways)])]
  transfers between devices with their start and end apart: 15 -> 22, of which waited for: 14 -> 19; matrix products, arithmetic and copies ran while one was open for 9% -> 10% of each run, Pallas kernels for 0% -> 0%
where the time goes in v1:
time: 815 us; the launch traced here: 814 us
  waiting for transfers between devices  622 us (76%)
  matrix products  70.5 us (9%)
  blocking collectives  35.7 us (4%)
  local copies, waits for them, and re-layouts  31.3 us (4%)
  other arithmetic  30.6 us (4%)
  between operations  14.7 us (2%)
  starting transfers between devices  8.87 us (1%)
    psum x1, waiting for transfers between devices, on_device(): mlp_sum = lax.psum(contract_last(hidden, down_full), 'tp')  154 us
    psum x1, waiting for transfers between devices, on_device(): back_two = lax.psum(contract_last(d_pre_bf, up_back), 'tp')  86.6 us
    psum x1, waiting for transfers between devices, on_device(): proj_sum = lax.psum(contract_last(attended, out_full), 'tp')  57.6 us
    reduce_scatter x1, waiting for transfers between devices, on_device(): lax.psum_scatter(grad_up, ('shard', 'ctx'), scatter_dimension=0, tiled=True)  55.5 us
    reduce_scatter x1, waiting for transfers between devices, on_device(): lax.psum_scatter(grad_down, ('shard', 'ctx'), scatter_dimension=0, tiled=...  55.1 us
    reduce_scatter x1, waiting for transfers between devices, on_device(): lax.psum_scatter(grad_qkv, ('shard', 'ctx'), scatter_dimension=1, tiled=T...  41.5 us
    reduce_scatter x1, waiting for transfers between devices, on_device(): lax.psum_scatter(grad_out, ('shard', 'ctx'), scatter_dimension=0, tiled=T...  38.2 us
    reduce_scatter x1, waiting for transfers between devices, on_device(): lax.psum_scatter(value_terms.reshape(groups, seq_len, head_width), 'ctx',...  30.6 us
  transfers between devices with their start and end apart: 22, of which 19 were waited for; matrix products, arithmetic and copies ran while one was open for 10% of the time, Pallas kernels for 0%

profile of v1, /device:TPU:0, one launch (start us, length us, event | category | flops | bytes accessed | tf_op | source)
XLA Modules:
  0.0 814.1 jit_solution(11472103905745986510)
XLA Ops:
  11.3 10.3 %all_gather.27 = bf16[6,1024]{1,0:T(8,128)(2,1)S(1)} all-gather(bf16[6,128]{1,0:T(8,128)(2,1)S(1)} %stack.61), channel_id=1, replica_groups=mesh['shard'=2,'ctx'=4,'tp'=4] {'shard','ctx'}, dimensions={1}, use_global_device_ids=true | all-gather | bytes 13824 | tf_op jit(solution)/shard_map/all_gather | solution.py:95
  22.2 16.3 %all-gather.6.cloned.1.call-done = bf16[3,1024,256]{2,1,0:T(8,128)(2,1)} async-done(((bf16[3,128,256]{2,1,0:T(8,128)(2,1)}), bf16[3,1024,256]{2,1,0:T(8,128)(2,1)}) %all-gather.6.cloned.1.call-update) | async-done | bytes 1572880 | tf_op jit(solution)/shard_map/all_gather | solution.py:91
  38.4 2.4 convolution_bitcast_fusion.2
  42.9 10.9 %all_gather.31 = bf16[1024,256]{1,0:T(8,128)(2,1)} all-gather(bf16[128,256]{1,0:T(8,128)(2,1)S(1)} %copy-done.25), channel_id=1, replica_groups=mesh['shard'=2,'ctx'=4,'tp'=4] {'shard','ctx'}, dimensions={0}, use_global_device_ids=true | all-gather | bytes 589824 | tf_op jit(solution)/shard_map/all_gather | solution.py:92
  56.1 2.0 add_convert_fusion.2
  63.0 3.0 select_reduce_fusion
  66.2 12.3 %all-gather.8.cloned.1.call-done = bf16[2,1024,256]{2,1,0:T(8,128)(2,1)} async-done(((bf16[2,256,256]{2,1,0:T(8,128)(2,1)}), bf16[2,1024,256]{2,1,0:T(8,128)(2,1)}) %all-gather.8.cloned.1.call-update) | async-done | bytes 1048592 | tf_op jit(solution)/shard_map/all_gather | solution.py:133
  80.0 6.0 fusion.31
  90.1 2.4 collective-permute-start.1
  92.6 4.2 collective-permute-done
  98.0 2.6 collective-permute-start.3
  105.8 2.7 collective-permute-start.5
  112.8 4.7 collective-permute-done.6
  117.6 57.6 %all-reduce.6.cloned.1.call-done = f32[512,1024]{1,0:T(8,128)} async-done(((f32[512,1024]{1,0:T(8,128)}), f32[512,1024]{1,0:T(8,128)}) %all-reduce.6.cloned.1.call-update) | async-done | bytes 2097168 | tf_op jit(solution)/shard_map/psum | solution.py:179
  175.2 1.9 fusion.54
  178.8 2.7 fusion.52
  181.4 22.6 %all-gather.12.cloned.1.call-done = bf16[1024,1024]{1,0:T(8,128)(2,1)} async-done(((bf16[128,1024]{1,0:T(8,128)(2,1)}), bf16[1024,1024]{1,0:T(8,128)(2,1)}) %all-gather.12.cloned.1.call-update) | async-done | bytes 2097168 | tf_op jit(solution)/shard_map/all_gather | solution.py:94
  204.0 5.9 fusion.60
  209.9 23.9 %all-gather.14.cloned.1.call-done = bf16[1024,1024]{1,0:T(8,128)(2,1)} async-done(((bf16[128,1024]{1,0:T(8,128)(2,1)}), bf16[1024,1024]{1,0:T(8,128)(2,1)}) %all-gather.14.cloned.1.call-update) | async-done | bytes 2097168 | tf_op jit(solution)/shard_map/all_gather | solution.py:193
  233.8 4.5 fusion.39
  238.4 86.6 %all-reduce.8.cloned.1.call-done = f32[512,1024]{1,0:T(8,128)} async-done(((f32[512,1024]{1,0:T(8,128)}), f32[512,1024]{1,0:T(8,128)}) %all-reduce.8.cloned.1.call-update) | async-done | bytes 2097168 | tf_op jit(solution)/shard_map/psum | solution.py:205
  325.0 2.6 multiply_reduce_fusion
  331.2 2.0 reshape.250
  333.3 2.0 copy.58
  336.4 6.1 multiply_convert_fusion
  342.5 2.6 convolution_multiply_fusion
  345.4 6.7 fusion.2
  352.3 5.3 fusion.51
  357.6 2.1 fusion.57
  359.7 2.0 copy.70
  361.7 2.2 reshape.249
  363.9 11.8 %reduce-scatter.8.cloned.1.call-done = f32[2,256,256]{1,2,0:T(8,128)} async-done(((f32[2,1024,256]{1,2,0:T(8,128)}), f32[2,256,256]{1,2,0:T(8,128)}) %reduce-scatter.8.cloned.1.call-update) | async-done | bytes 524304 | tf_op jit(solution)/shard_map/reduce_scatter | solution.py:250
  379.2 30.6 %reduce-scatter.10.cloned.1.call-done = f32[2,256,256]{1,2,0:T(8,128)} async-done(((f32[2,1024,256]{1,2,0:T(8,128)}), f32[2,256,256]{1,2,0:T(8,128)}) %reduce-scatter.10.cloned.1.call-update) | async-done | bytes 524304 | tf_op jit(solution)/shard_map/reduce_scatter | solution.py:253
  409.9 2.0 fusion.58
  413.6 4.0 convolution_bitcast_fusion.1
  419.3 153.9 %all-reduce.10.cloned.1.call-done = (f32[512,1024]{1,0:T(8,128)}, f32[512,1024]{1,0:T(8,128)}) async-done(((f32[512,1024]{1,0:T(8,128)}, f32[512,1024]{1,0:T(8,128)}), (f32[512,1024]{1,0:T(8,128)}, f32[512,1024]{1,0:T(8,128)})) %all-reduce.10.cloned.1.call-update) | async-done | bytes 4194320 | tf_op jit(solution)/shard_map/psum | solution.py:188
  573.2 2.5 fusion.26
  576.4 4.2 convolution_bitcast_fusion
  580.8 3.1 fusion.34
  583.9 4.6 fusion.37
  588.6 5.3 fusion.50
  594.1 14.4 %all-reduce = (f32[2,256]{1,0:T(2,128)}, f32[1024]{0:T(1024)}) all-reduce(f32[2,256]{1,0:T(2,128)S(1)} %pad_maximum_fusion.3, f32[1024]{0:T(1024)S(1)} %get-tuple-element.95), channel_id=1, replica_groups=mesh['shard'=2,'ctx'=4,'tp'=4] {'shard','ctx'}, use_global_device_ids=true, to_apply=%region_27.28 | all-reduce | flops 1536 | bytes 12288 | tf_op jit(solution)/shard_map/psum | solution.py:289
  608.5 3.3 add_select_fusion
  611.8 2.0 fusion.25
  615.3 41.5 %reduce-scatter.14.cloned.1.call-done = f32[3,128,256]{1,2,0:T(8,128)} async-done(((f32[3,1024,256]{1,2,0:T(8,128)}), f32[3,128,256]{1,2,0:T(8,128)}) %reduce-scatter.14.cloned.1.call-update) | async-done | bytes 393232 | tf_op jit(solution)/shard_map/reduce_scatter | solution.py:282
  658.7 38.2 %reduce-scatter.16.cloned.1.call-done = f32[128,256]{1,0:T(8,128)} async-done(((f32[1024,256]{1,0:T(8,128)}), f32[128,256]{1,0:T(8,128)}) %reduce-scatter.16.cloned.1.call-update) | async-done | bytes 131088 | tf_op jit(solution)/shard_map/reduce_scatter | solution.py:283
  697.0 55.5 %reduce-scatter.18.cloned.1.call-done = f32[128,1024]{1,0:T(8,128)} async-done(((f32[1024,1024]{1,0:T(8,128)}), f32[128,1024]{1,0:T(8,128)}) %reduce-scatter.18.cloned.1.call-update) | async-done | bytes 524304 | tf_op jit(solution)/shard_map/reduce_scatter | solution.py:284
  752.5 55.1 %reduce-scatter.20.cloned.1.call-done = f32[128,1024]{1,0:T(8,128)} async-done(((f32[1024,1024]{1,0:T(8,128)}), f32[128,1024]{1,0:T(8,128)}) %reduce-scatter.20.cloned.1.call-update) | async-done | bytes 524304 | tf_op jit(solution)/shard_map/reduce_scatter | solution.py:285
  (170 shorter events, 47.8 us)
Async XLA Ops:
  7.2 14.5 %copy-start = (bf16[2,256,1024]{2,1,0:T(8,128)(2,1)S(1)}, bf16[2,256,1024]{2,1,0:T(8,128)(2,1)}, u32[]{:S(2)}) copy-start(bf16[2,256,1024]{2,1,0:T(8,128)(2,1)} %param.15) | copy-start | bytes 3145732
  7.2 4.0 copy-start.29
  7.2 4.0 copy-start.30
  7.2 4.0 copy-start.31
  7.2 4.0 copy-start.32
  7.2 4.0 copy-start.33
  7.2 4.0 copy-start.34
  7.3 14.4 %copy-start.26 = (bf16[2,256]{1,0:T(2,128)(2,1)S(1)}, bf16[2,256]{1,0:T(2,128)(2,1)}, u32[]{:S(2)}) copy-start(bf16[2,256]{1,0:T(2,128)(2,1)} %param.21) | copy-start | bytes 3076
  7.3 31.2 %all-gather.6.cloned.1.call-start = ((), (), s32[]{:S(2)}) async-start(), calls=%async_computation.7 | async-start | bytes 1769472 | tf_op jit(solution)/shard_map/all_gather | solution.py:91
  8.0 51.6 %all-gather.10.cloned.1.call-start = ((), (), s32[]{:S(2)}) async-start(), calls=%async_computation.9 | async-start | bytes 1310720 | tf_op jit(solution)/shard_map/all_gather | solution.py:132
  22.1 18.7 %copy-start.22 = (bf16[512,1024]{1,0:T(8,128)(2,1)}, bf16[512,1024]{1,0:T(8,128)(2,1)S(1)}, u32[]{:S(2)}) copy-start(bf16[512,1024]{1,0:T(8,128)(2,1)S(1)} %fusion.21) | copy-start | bytes 3145732
  22.1 20.7 %copy-start.25 = (bf16[128,256]{1,0:T(8,128)(2,1)S(1)}, bf16[128,256]{1,0:T(8,128)(2,1)}, u32[]{:S(2)}) copy-start(bf16[128,256]{1,0:T(8,128)(2,1)} %param.22) | copy-start | bytes 196612
  22.1 31.6 %copy-start.28 = (s32[2]{0:T(128)S(1)}, s32[2]{0:T(128)}, u32[]{:S(2)}) copy-start(s32[2]{0:T(128)} %param.16) | copy-start | bytes 28
  42.7 35.8 %all-gather.8.cloned.1.call-start = ((), (), s32[]{:S(2)}) async-start(), calls=%async_computation.8 | async-start | bytes 1310720 | tf_op jit(solution)/shard_map/all_gather | solution.py:133
  42.9 11.5 %copy-start.20 = (f32[3,512,256]{2,1,0:T(8,128)S(1)}, f32[3,512,256]{2,1,0:T(8,128)}, u32[]{:S(2)}) copy-start(f32[3,512,256]{2,1,0:T(8,128)} %copy-done.19) | copy-start | bytes 4718596
  54.3 25.7 %copy-start.14 = (pred[2,256,1024]{2,1,0:T(8,128)(4,1)}, pred[2,256,1024]{2,1,0:T(8,128)(4,1)S(1)}, u32[]{:S(2)}) copy-start(pred[2,256,1024]{2,1,0:T(8,128)(4,1)S(1)} %broadcast_and_fusion) | copy-start | bytes 1572868
  56.1 6.9 copy-start.12
  58.1 117.1 %all-reduce.6.cloned.1.call-start = ((), (), s32[]{:S(2)}) async-start(), calls=%async_computation.10 | async-start | bytes 4194304 | tf_op jit(solution)/shard_map/psum | solution.py:179
  63.0 3.2 copy-start.1
  80.0 6.0 copy-start.23
  80.0 6.7 copy-start.15
  86.7 3.1 copy-start.21
  86.7 10.0 %copy-start.6 = (bf16[2,256,1024]{2,1,0:T(8,128)(2,1)S(1)}, bf16[2,256,1024]{2,1,0:T(8,128)(2,1)}, u32[]{:S(2)}) copy-start(bf16[2,256,1024]{2,1,0:T(8,128)(2,1)} %param.17) | copy-start | bytes 3145732
  88.6 115.4 %all-gather.12.cloned.1.call-start = ((), (), s32[]{:S(2)}) async-start(), calls=%async_computation.11 | async-start | bytes 2359296 | tf_op jit(solution)/shard_map/all_gather | solution.py:94
  89.2 144.7 %all-gather.14.cloned.1.call-start = ((), (), s32[]{:S(2)}) async-start(), calls=%async_computation.12 | async-start | bytes 2359296 | tf_op jit(solution)/shard_map/all_gather | solution.py:193
  89.7 235.3 %all-reduce.8.cloned.1.call-start = ((), (), s32[]{:S(2)}) async-start(), calls=%async_computation.13 | async-start | bytes 4194304 | tf_op jit(solution)/shard_map/psum | solution.py:205
  89.8 7.0 collective-permute-start
  90.1 7.9 collective-permute-start.1
  92.6 9.4 %copy-start.27 = (bf16[1024]{0:T(1024)(128)(2,1)S(1)}, bf16[1024]{0:T(1024)(128)(2,1)}, u32[]{:S(2)}) copy-start(bf16[1024]{0:T(1024)(128)(2,1)} %param.27) | copy-start | bytes 6148
  96.8 7.1 collective-permute-start.2
  98.0 7.9 collective-permute-start.3
  103.9 7.0 collective-permute-start.4
  105.8 6.9 collective-permute-start.5
  110.9 6.7 collective-permute-start.6
  117.6 57.7 %copy-start.17 = (bf16[1024,1024]{1,0:T(8,128)(2,1)}, bf16[1024,1024]{1,0:T(8,128)(2,1)S(1)}, u32[]{:S(2)}) copy-start(bf16[1024,1024]{1,0:T(8,128)(2,1)S(1)} %constant_dynamic-update-slice_fusion) | copy-start | bytes 6291460
  238.4 137.3 %reduce-scatter.8.cloned.1.call-start = ((), (), s32[]{:S(2)}) async-start(), calls=%async_computation.14 | async-start | bytes 2621440 | tf_op jit(solution)/shard_map/reduce_scatter | solution.py:250
  336.3 6.1 copy-start.13
  345.1 64.7 %reduce-scatter.10.cloned.1.call-start = ((), (), s32[]{:S(2)}) async-start(), calls=%async_computation.15 | async-start | bytes 2621440 | tf_op jit(solution)/shard_map/reduce_scatter | solution.py:253
  352.2 221.0 %all-reduce.10.cloned.1.call-start = ((), (), s32[]{:S(2)}) async-start(), calls=%async_computation.21 | async-start | bytes 8388608 | tf_op jit(solution)/shard_map/psum | solution.py:188
  352.2 5.4 copy-start.5
  352.3 5.4 copy-start.9
  417.7 196.2 %reduce-scatter.12.cloned.1.call-start = ((), (), s32[]{:S(2)}) async-start(), calls=%async_computation.16 | async-start | bytes 36864 | tf_op jit(solution)/shard_map/reduce_scatter | solution.py:286
  576.4 80.5 %reduce-scatter.14.cloned.1.call-start = ((), (), s32[]{:S(2)}) async-start(), calls=%async_computation.17 | async-start | bytes 3538944 | tf_op jit(solution)/shard_map/reduce_scatter | solution.py:282
  580.7 116.3 %reduce-scatter.16.cloned.1.call-start = ((), (), s32[]{:S(2)}) async-start(), calls=%async_computation.18 | async-start | bytes 1179648 | tf_op jit(solution)/shard_map/reduce_scatter | solution.py:283
  583.9 168.6 %reduce-scatter.18.cloned.1.call-start = ((), (), s32[]{:S(2)}) async-start(), calls=%async_computation.19 | async-start | bytes 4718592 | tf_op jit(solution)/shard_map/reduce_scatter | solution.py:284
  588.5 219.1 %reduce-scatter.20.cloned.1.call-start = ((), (), s32[]{:S(2)}) async-start(), calls=%async_computation.20 | async-start | bytes 4718592 | tf_op jit(solution)/shard_map/reduce_scatter | solution.py:285
  608.5 3.3 copy-start.3
  608.5 3.3 copy-start.11
  (9 other events, 16.9 us)
Sparse Core Ops, SparseCore 0:
  10.0 28.3 all-gather.5
  42.8 16.7 all-gather.9
  61.8 16.7 all-gather.7
  88.7 86.4 all-reduce.5
  177.1 26.8 all-gather.11
  205.9 27.8 all-gather.13
  238.5 86.4 all-reduce.7
  345.3 30.3 reduce-scatter.7
  378.4 31.4 reduce-scatter.9
  417.8 155.3 all-reduce.9
  577.0 30.2 reduce-scatter.11
  610.6 46.2 reduce-scatter.13
  660.9 36.0 reduce-scatter.15
  701.1 51.2 reduce-scatter.17
  756.2 51.3 reduce-scatter.19
